TPU v7x, 32 devices: a whole 2x2x4 slice. The times are simulated.
32 devices in a mesh: front: 8 (over z, core), tile: 4 (over y, x).
Axes of the slice: x: 2, y: 2, z: 4, core: 2. Of those that a mesh axis runs over, the one named last changes fastest.
Arguments:
- child_rhs: float32 [8, 2048, 256], P('front', 'tile'), may hold values from -6 to 6
- child_lower: float32 [8, 2048, 2048], P('front', 'tile'), as said below
- child_border: float32 [8, 2048, 2048], P('front', 'tile'), may hold values from -0.125 to 0.125
- child_upper_border: float32 [8, 2048, 2048], P('front', 'tile'), may hold values from -0.125 to 0.125
- child_upper: float32 [8, 2048, 2048], P('front', 'tile'), as said below
- parent_rhs: float32 [8, 512, 256], P('front', 'tile'), may hold values from -6 to 6
- parent_lower: float32 [8, 512, 2048], P('front', 'tile'), as said below
- parent_upper: float32 [8, 512, 2048], P('front', 'tile'), as said below
- border_map: int32 [8, 2048], P('front'), may hold values from 0 to 2047, as said below
- border_count: int32 [8], P('front'), may hold values from 512 to 2048, as said below
Outputs:
- child_solution: float32 [8, 2048, 256], P('front', 'tile')
- parent_solution: float32 [8, 512, 256], P('front', 'tile')
Inputs may be any that keep to these rules, and one draw needn't show every extreme that they name: `border_map`: within one child the 2048 entries are distinct parent rows. Group g of parent rows holds the rows m with (m mod (512)) // 128 = g, for g below 4. In every aligned block of 512 border rows of a child, each group receives either no row or exactly 256 rows, and each group receives 2048 // 4 border rows of the child in all. `border_count`: some child has all 2048 border rows live. `child_lower`: lower triangular including the diagonal. `child_upper`: upper triangular including the diagonal. `parent_lower`: each parent's 2048 rows form a lower triangular matrix including the diagonal. `parent_upper`: each parent's 2048 rows form an upper triangular matrix including the diagonal.
All inputs are finite; a program needn't handle non-finite values.
Results may differ from a plain program's by a relative error of at most 0.00013.
Values sent between devices are 32-bit elements; how exact they have to be, the bound alone decides.
A program may use at most 64 MiB of HBM per device.

v0:
```python
import jax
import jax.numpy as jnp
from jax import lax
from jax.sharding import PartitionSpec as P


def partner_2(block, axis, apart):
    count = lax.axis_size(axis)
    route = []
    for low in range(count):
        high = low | 1 << apart
        if high != low and high < count:
            route += [(low, high), (high, low)]
    return lax.ppermute(block, axis, route)


def product(matrix, vector):
    return jnp.dot(
        matrix, vector, preferred_element_type=jnp.float32, precision=lax.Precision.HIGHEST
    )


def apply_rows(matrix, local_rows):
    return product(matrix, lax.all_gather(local_rows, "tile", axis=0, tiled=True))


def pair_quarters(stacked, quarter):
    for bit_number in (0, 1):
        partner = partner_2(stacked, "front", bit_number)
        upper_bit = jnp.right_shift(quarter, bit_number) % 2
        stacked = jnp.where(
            upper_bit == 0,
            jnp.concatenate([stacked, partner], 0),
            jnp.concatenate([partner, stacked], 0),
        )
    return stacked


def assemble(block, quarter):
    whole_quarter = lax.all_gather(block, "tile", axis=0, tiled=True)
    stacked = pair_quarters(whole_quarter[None], quarter)
    return stacked.reshape(-1, block.shape[1])


def layout_index(parent_row, quarter_rows, slab_rows):
    return (
        parent_row % quarter_rows // slab_rows * (4 * slab_rows)
        + parent_row // quarter_rows * slab_rows
        + parent_row % slab_rows
    )


def local(
    child_rhs,
    child_lower,
    child_border,
    child_upper_border,
    child_upper,
    parent_rhs,
    parent_lower,
    parent_upper,
    border_map,
    border_count,
):
    tile_pos = lax.axis_index("tile")
    quarter = lax.axis_index("front") % 4
    border_rows = child_border.shape[1]
    slab_rows = parent_lower.shape[1]
    parent_rows = parent_lower.shape[2]
    quarter_rows = parent_rows // 4
    slab_width = 4 * slab_rows
    live_total = border_count[0]
    map_whole = border_map[0]
    forward_child = apply_rows(child_lower[0], child_rhs[0])
    own_ids = tile_pos * border_rows + jnp.arange(border_rows, dtype=jnp.int32)
    own_map = lax.dynamic_slice_in_dim(map_whole, tile_pos * border_rows, border_rows, 0)
    alive_rows = own_ids < live_total
    update = -apply_rows(child_border[0], forward_child)
    update = jnp.where(alive_rows[:, None], update, 0.0)
    target = layout_index(own_map, quarter_rows, slab_rows)
    target = jnp.where(alive_rows, target, -1)
    row_ids = jnp.arange(slab_width * lax.axis_size("tile"), dtype=jnp.int32)
    selector = (row_ids[:, None] == target[None, :]).astype(jnp.float32)
    scattered = lax.psum_scatter(product(selector, update), "tile", scatter_dimension=0, tiled=True)
    stacked = scattered.reshape(4, slab_rows, scattered.shape[1])
    for bit_number in (1, 0):
        half_size = stacked.shape[0] // 2
        upper_bit = jnp.right_shift(quarter, bit_number) % 2
        retained = lax.dynamic_slice_in_dim(stacked, upper_bit * half_size, half_size, 0)
        sending = lax.dynamic_slice_in_dim(stacked, (1 - upper_bit) * half_size, half_size, 0)
        stacked = retained + partner_2(sending, "front", bit_number)
    gathered = stacked[0]
    right_parent = parent_rhs[0] + gathered
    forward_parent = product(parent_lower[0], assemble(right_parent, quarter))
    solved_parent = product(parent_upper[0], assemble(forward_parent, quarter))
    parent_whole = assemble(solved_parent, quarter)
    selector = (
        (own_map[:, None] == jnp.arange(parent_rows, dtype=jnp.int32)[None, :])
        & alive_rows[:, None]
    ).astype(jnp.float32)
    border_values = product(selector, parent_whole)
    reduced = forward_child - apply_rows(child_upper_border[0], border_values)
    child_solution = apply_rows(child_upper[0], reduced)
    return (child_solution[None], solved_parent[None])


def solution(mesh):
    return jax.shard_map(
        local,
        mesh=mesh,
        in_specs=(
            P("front", "tile", None),
            P("front", "tile", None),
            P("front", "tile", None),
            P("front", "tile", None),
            P("front", "tile", None),
            P("front", "tile", None),
            P("front", "tile", None),
            P("front", "tile", None),
            P("front", None),
            P("front"),
        ),
        out_specs=(P("front", "tile", None), P("front", "tile", None)),
        check_vma=False,
    )
```

profile of v0, /device:TPU:0, one launch (start us, length us, event | category | flops | bytes accessed | tf_op | source)
XLA Modules:
  0.0 388.4 jit_solution(4923493146791884085)
XLA Ops:
  7.2 0.0 copy-start
  7.2 0.0 all-gather.13.cloned.1.call-start
  7.2 0.7 all-gather.13.cloned.1.call-update
  7.9 0.0 all-gather.7.cloned.1.call-start
  8.0 39.9 %all-gather.13.cloned.1.call-done = f32[1,2048,256]{2,1,0:T(8,128)} async-done(((f32[1,512,256]{2,1,0:T(8,128)}), f32[1,2048,256]{2,1,0:T(8,128)}) %all-gather.13.cloned.1.call-update) | async-done | bytes 2097168 | tf_op jit(solution)/shard_map/all_gather | solution.py:24
  47.9 7.1 %fusion.6 = f32[512,256]{1,0:T(8,128)} fusion(f32[1,512,2048]{2,1,0:T(8,128)} %param.11, f32[1,2048,256]{2,1,0:T(8,128)} %all-gather.13.cloned.1.call-done), kind=kOutput, calls=%fused_computation.6 | convolution fusion | flops 3221225472 | bytes 6815744 | tf_op jit(solution)/shard_map/dot_general | solution.py:18
  55.0 0.0 all-gather.7.cloned.1.call-update
  55.0 0.0 reduce-scatter.2.cloned.1.call-start
  55.7 0.7 compare_select_fusion
  56.5 34.0 %all-gather.7.cloned.1.call-done = f32[2048,256]{1,0:T(8,128)} async-done(((f32[512,256]{1,0:T(8,128)}), f32[2048,256]{1,0:T(8,128)}) %all-gather.7.cloned.1.call-update) | async-done | bytes 2097168 | tf_op jit(solution)/shard_map/all_gather | solution.py:24
  90.5 9.3 %fusion.19 = f32[256,512]{1,0:T(8,128)S(1)} fusion(f32[2048,256]{1,0:T(8,128)} %all-gather.7.cloned.1.call-done, f32[1,512,2048]{2,1,0:T(8,128)} %param.12, pred[512]{0:T(512)(128)(4,1)S(1)} %add_compare_fusion), kind=kOutput, calls=%fused_computation.21 | convolution fusion | flops 3221487616 | bytes 6816256 | tf_op jit(solution)/shard_map/dot_general | solution.py:18
  99.8 3.3 fusion.11
  103.1 0.0 reduce-scatter.2.cloned.1.call-update
  103.1 0.0 copy-start.3
  103.1 0.0 all-gather.9.cloned.1.call-start
  103.2 35.3 %reduce-scatter.2.cloned.1.call-done = f32[512,256]{1,0:T(8,128)} async-done(((f32[2048,256]{1,0:T(8,128)}), f32[512,256]{1,0:T(8,128)}) %reduce-scatter.2.cloned.1.call-update) | async-done | bytes 524304 | tf_op jit(solution)/shard_map/reduce_scatter | solution.py:84
  138.5 1.1 constant_dynamic-slice_fusion.1
  139.6 0.1 copy.26
  139.7 1.6 collective-permute-start
  141.2 0.1 copy.25
  141.4 6.4 %collective-permute-done = f32[2,128,256]{1,2,0:T(8,128)S(1)} collective-permute-done((f32[2,128,256]{1,2,0:T(8,128)S(1)}, f32[2,128,256]{1,2,0:T(8,128)S(1)}, u32[]{:S(2)}, u32[]{:S(2)}) %collective-permute-start) | collective-permute-done | bytes 262176 | tf_op jit(solution)/shard_map/ppermute | solution.py:14
  147.9 0.1 collective-permute-start.1
  147.9 0.0 copy-done.3
  148.0 0.1 copy.19
  148.1 1.2 collective-permute-done.1
  149.3 14.2 %all-gather.1 = f32[1,512,256]{1,2,0:T(8,128)S(1)} all-gather(f32[1,128,256]{1,2,0:T(8,128)S(1)} %add_add_fusion), channel_id=3, replica_groups=mesh['front'=8,'tile'=4] {'tile'}, dimensions={1}, use_global_device_ids=true | all-gather | bytes 655360 | tf_op jit(solution)/shard_map/all_gather | solution.py:40
  163.5 0.0 collective-permute-start.2
  163.5 1.9 collective-permute-done.2
  165.5 0.1 maximum_select_fusion.3
  165.6 0.0 copy-start.2
  165.6 1.6 collective-permute-start.3
  167.1 0.0 copy-done.2
  167.1 23.8 %collective-permute-done.3 = f32[2,512,256]{1,2,0:T(8,128)} collective-permute-done((f32[2,512,256]{1,2,0:T(8,128)S(1)}, f32[2,512,256]{1,2,0:T(8,128)}, u32[]{:S(2)}, u32[]{:S(2)}) %collective-permute-start.3) | collective-permute-done | bytes 1048608 | tf_op jit(solution)/shard_map/ppermute | solution.py:14
  191.0 2.7 maximum_select_fusion
  193.6 1.8 copy.20
  195.5 0.0 copy-done
  195.5 5.0 %convolution_bitcast_fusion = f32[128,256]{0,1:T(8,128)S(1)} fusion(f32[2048,256]{1,0:T(8,128)} %bitcast.62, f32[1,128,2048]{2,1,0:T(8,128)S(1)} %copy-done), kind=kOutput, calls=%fused_computation.25 | convolution fusion | flops 805306368 | bytes 3276800 | tf_op jit(solution)/shard_map/dot_general | solution.py:18
  200.5 11.5 %all_gather.24 = f32[512,256]{0,1:T(8,128)S(1)} all-gather(f32[128,256]{0,1:T(8,128)S(1)} %convolution_bitcast_fusion), channel_id=1, replica_groups=mesh['front'=8,'tile'=4] {'tile'}, dimensions={0}, use_global_device_ids=true | all-gather | bytes 655360 | tf_op jit(solution)/shard_map/all_gather | solution.py:40
  212.0 0.0 collective-permute-start.4
  212.0 1.9 collective-permute-done.4
  213.9 0.1 maximum_select_fusion.4
  214.1 1.6 collective-permute-start.5
  215.6 23.7 %collective-permute-done.5 = f32[2,512,256]{1,2,0:T(8,128)S(1)} collective-permute-done((f32[2,512,256]{1,2,0:T(8,128)S(1)}, f32[2,512,256]{1,2,0:T(8,128)S(1)}, u32[]{:S(2)}, u32[]{:S(2)}) %collective-permute-start.5) | collective-permute-done | bytes 1048608 | tf_op jit(solution)/shard_map/ppermute | solution.py:14
  239.3 0.2 maximum_select_fusion.1
  239.6 1.8 copy.21
  241.4 5.3 %fusion.31 = f32[256,128]{1,0:T(8,128)S(1)} fusion(f32[2048,256]{1,0:T(8,128)} %bitcast.63, f32[1,128,2048]{2,1,0:T(8,128)} %param.17), kind=kOutput, calls=%fused_computation.29 | convolution fusion | flops 805306368 | bytes 3276800 | tf_op jit(solution)/shard_map/dot_general | solution.py:18
  246.7 12.5 %all_gather.25 = f32[512,256]{0,1:T(8,128)S(1)} all-gather(f32[128,256]{0,1:T(8,128)S(1)} %bitcast.69), channel_id=1, replica_groups=mesh['front'=8,'tile'=4] {'tile'}, dimensions={0}, use_global_device_ids=true | all-gather | bytes 655360 | tf_op jit(solution)/shard_map/all_gather | solution.py:40
  259.2 0.0 collective-permute-start.6
  259.2 1.9 collective-permute-done.6
  261.1 0.1 maximum_select_fusion.5
  261.2 1.6 collective-permute-start.7
  262.8 23.7 %collective-permute-done.7 = f32[2,512,256]{1,2,0:T(8,128)S(1)} collective-permute-done((f32[2,512,256]{1,2,0:T(8,128)S(1)}, f32[2,512,256]{1,2,0:T(8,128)S(1)}, u32[]{:S(2)}, u32[]{:S(2)}) %collective-permute-start.7) | collective-permute-done | bytes 1048608 | tf_op jit(solution)/shard_map/ppermute | solution.py:14
  286.5 0.2 maximum_select_fusion.2
  286.8 1.8 copy.22
  288.6 4.9 %fusion.9 = f32[512,256]{1,0:T(8,128)} fusion(f32[2048,256]{1,0:T(8,128)} %bitcast.68, s32[512]{0:T(512)S(1)} %bitcast.72, pred[512]{0:T(512)(128)(4,1)S(1)} %add_compare_fusion), kind=kOutput, calls=%fused_computation.11 | convolution fusion | flops 3223322624 | bytes 2624000 | tf_op jit(solution)/shard_map/dot_general | solution.py:18
  293.5 0.0 all-gather.9.cloned.1.call-update
  293.5 0.0 all-gather.11.cloned.1.call-start
  293.5 35.4 %all-gather.9.cloned.1.call-done = f32[2048,256]{1,0:T(8,128)} async-done(((f32[512,256]{1,0:T(8,128)}), f32[2048,256]{1,0:T(8,128)}) %all-gather.9.cloned.1.call-update) | async-done | bytes 2097168 | tf_op jit(solution)/shard_map/all_gather | solution.py:24
  329.0 7.1 %fusion.28 = f32[512,256]{1,0:T(8,128)} fusion(f32[512,256]{1,0:T(8,128)S(1)} %copy-done.1, f32[2048,256]{1,0:T(8,128)} %all-gather.9.cloned.1.call-done, f32[1,512,2048]{2,1,0:T(8,128)} %param.13), kind=kOutput, calls=%fused_computation.24 | convolution fusion | flops 3221356544 | bytes 7340032 | tf_op jit(solution)/shard_map/dot_general | solution.py:18
  336.1 0.0 all-gather.11.cloned.1.call-update
  336.1 0.8 copy.24
  336.9 34.7 %all-gather.11.cloned.1.call-done = f32[2048,256]{1,0:T(8,128)} async-done(((f32[512,256]{1,0:T(8,128)}), f32[2048,256]{1,0:T(8,128)}) %all-gather.11.cloned.1.call-update) | async-done | bytes 2097168 | tf_op jit(solution)/shard_map/all_gather | solution.py:24
  371.6 9.3 %fusion.25 = f32[1,512,256]{1,2,0:T(8,128)S(1)} fusion(f32[2048,256]{1,0:T(8,128)} %all-gather.11.cloned.1.call-done, f32[1,512,2048]{2,1,0:T(8,128)} %param.14), kind=kOutput, calls=%fused_computation.23 | convolution fusion | flops 3221225472 | bytes 6815744 | tf_op jit(solution)/shard_map/dot_general | solution.py:18
  380.9 1.0 copy.23
  (6 shorter events, 0.1 us)
Async XLA Ops:
  7.2 188.3 %copy-start = (f32[1,128,2048]{2,1,0:T(8,128)S(1)}, f32[1,128,2048]{2,1,0:T(8,128)}, u32[]{:S(2)}) copy-start(f32[1,128,2048]{2,1,0:T(8,128)} %param.16) | copy-start | bytes 3145732
  7.2 40.7 %all-gather.13.cloned.1.call-start = ((), (), s32[]{:S(2)}) async-start(), calls=%async_computation.5 | async-start | bytes 2621440 | tf_op jit(solution)/shard_map/all_gather | solution.py:24
  7.9 82.6 %all-gather.7.cloned.1.call-start = ((), (), s32[]{:S(2)}) async-start(), calls=%async_computation.1 | async-start | bytes 2621440 | tf_op jit(solution)/shard_map/all_gather | solution.py:24
  55.0 83.5 %reduce-scatter.2.cloned.1.call-start = ((), (), s32[]{:S(2)}) async-start(), calls=%async_computation.2 | async-start | bytes 2621440 | tf_op jit(solution)/shard_map/reduce_scatter | solution.py:84
  103.1 44.8 %copy-start.3 = (f32[1,128,256]{2,1,0:T(8,128)S(1)}, f32[1,128,256]{2,1,0:T(8,128)}, u32[]{:S(2)}) copy-start(f32[1,128,256]{2,1,0:T(8,128)} %param.15) | copy-start | bytes 393220
  103.1 225.8 %all-gather.9.cloned.1.call-start = ((), (), s32[]{:S(2)}) async-start(), calls=%async_computation.3 | async-start | bytes 2621440 | tf_op jit(solution)/shard_map/all_gather | solution.py:24
  139.7 8.1 %collective-permute-start = (f32[2,128,256]{1,2,0:T(8,128)S(1)}, f32[2,128,256]{1,2,0:T(8,128)S(1)}, u32[]{:S(2)}, u32[]{:S(2)}) collective-permute-start(f32[2,128,256]{1,2,0:T(8,128)S(1)} %copy.26), channel_id=1, source_target_pairs={{0,8},{8,0},{4,12},{12,4},{16,24},{24,16},{20,28},{28,20},{1,9},{9... | collective-permute-start | bytes 786440 | tf_op jit(solution)/shard_map/ppermute | solution.py:14
  147.9 1.4 collective-permute-start.1
  163.5 1.9 collective-permute-start.2
  165.6 1.6 copy-start.2
  165.6 25.4 %collective-permute-start.3 = (f32[2,512,256]{1,2,0:T(8,128)S(1)}, f32[2,512,256]{1,2,0:T(8,128)}, u32[]{:S(2)}, u32[]{:S(2)}) collective-permute-start(f32[2,512,256]{1,2,0:T(8,128)S(1)} %maximum_select_fusion.3), channel_id=1, source_target_pairs={{0,8},{8,0},{4,12},{12,4},{16,24},{24,16},{20,28},{28,20},{1,9},{9... | collective-permute-start | bytes 3145736 | tf_op jit(solution)/shard_map/ppermute | solution.py:14
  212.0 1.9 collective-permute-start.4
  214.1 25.3 %collective-permute-start.5 = (f32[2,512,256]{1,2,0:T(8,128)S(1)}, f32[2,512,256]{1,2,0:T(8,128)S(1)}, u32[]{:S(2)}, u32[]{:S(2)}) collective-permute-start(f32[2,512,256]{1,2,0:T(8,128)S(1)} %maximum_select_fusion.4), channel_id=1, source_target_pairs={{0,8},{8,0},{4,12},{12,4},{16,24},{24,16},{20,28},{28,20},{1,9},{9... | collective-permute-start | bytes 3145736 | tf_op jit(solution)/shard_map/ppermute | solution.py:14
  259.2 1.9 collective-permute-start.6
  261.2 25.3 %collective-permute-start.7 = (f32[2,512,256]{1,2,0:T(8,128)S(1)}, f32[2,512,256]{1,2,0:T(8,128)S(1)}, u32[]{:S(2)}, u32[]{:S(2)}) collective-permute-start(f32[2,512,256]{1,2,0:T(8,128)S(1)} %maximum_select_fusion.5), channel_id=1, source_target_pairs={{0,8},{8,0},{4,12},{12,4},{16,24},{24,16},{20,28},{28,20},{1,9},{9... | collective-permute-start | bytes 3145736 | tf_op jit(solution)/shard_map/ppermute | solution.py:14
  288.6 40.4 %copy-start.1 = (f32[512,256]{1,0:T(8,128)S(1)}, f32[512,256]{1,0:T(8,128)}, u32[]{:S(2)}) copy-start(f32[512,256]{1,0:T(8,128)} %fusion.6) | copy-start | bytes 1572868
  293.5 78.1 %all-gather.11.cloned.1.call-start = ((), (), s32[]{:S(2)}) async-start(), calls=%async_computation.4 | async-start | bytes 2621440 | tf_op jit(solution)/shard_map/all_gather | solution.py:24
Sparse Core Ops, SparseCore 0:
  9.9 38.0 all-gather.12
  55.1 35.3 all-gather.6
  103.3 35.1 reduce-scatter.1
  293.6 35.3 all-gather.8
  336.2 35.3 all-gather.10
where the time goes:
time: 389 us; the launch traced here: 388 us
  waiting for transfers between devices  265 us (68%)
  matrix products  51.3 us (13%)
  blocking collectives  38.3 us (10%)
  between operations  14.7 us (4%)
  local copies, waits for them, and re-layouts  8.67 us (2%)
  starting transfers between devices  6.48 us (2%)
  other arithmetic  4.29 us (1%)
    all_gather x4, waiting for transfers between devices, apply_rows(): lax.all_gather(local_rows, 'tile', axis=0, tiled=True)  144 us
    ppermute x8, waiting for transfers between devices, partner_2(): return lax.ppermute(block, axis, route)  84.6 us
    dot_general x8, matrix products, product(): jnp.dot(matrix, vector, preferred_element_type=jnp.float32, precision=lax...  51.3 us
    all_gather x3, blocking collectives, assemble(): whole_quarter = lax.all_gather(block, 'tile', axis=0, tiled=True)  38.3 us
    reduce_scatter x1, waiting for transfers between devices, local(): lax.psum_scatter(product(selector, update), 'tile', scatter_dimension=0,...  35.3 us
  transfers between devices with their start and end apart: 13, of which 13 were waited for; matrix products, arithmetic and copies ran while one was open for 0% of the time, Pallas kernels for 0%

commit v1 on v0

--- a/solution.py
+++ b/solution.py
@@ -2,6 +2,7 @@
 import jax.numpy as jnp
 from jax import lax
 from jax.sharding import PartitionSpec as P
+from jax.lax import axis_index, axis_size, ppermute
 
 
 def partner_2(block, axis, apart):
@@ -21,7 +22,38 @@
 
 
 def apply_rows(matrix, local_rows):
-    return product(matrix, lax.all_gather(local_rows, "tile", axis=0, tiled=True))
+
+    def rails_return_all(block_here):
+        reached, carry_out, block_last = (
+            axis_size("tile"),
+            axis_index("tile"),
+            block_here.shape[0],
+        )
+        arrivals = list(map(lambda idx: (idx, (idx + 1) % reached), range(reached)))
+        cards = list(map(lambda idx: (idx, (idx - 1) % reached), range(reached)))
+        value_now = jnp.zeros(
+            (*block_here.shape[:0], reached * block_last, *block_here.shape[1:]), block_here.dtype
+        )
+        value_now = lax.dynamic_update_slice_in_dim(
+            value_now, block_here, carry_out * block_last, axis=0
+        )
+        v_next = y2 = block_here
+        s_next = reached // 2
+        no = 1
+        while no < s_next + 1:
+            v_next = ppermute(v_next, axis_name="tile", perm=arrivals)
+            value_now = lax.dynamic_update_slice_in_dim(
+                value_now, v_next, (carry_out - no) % reached * block_last, axis=0
+            )
+            if no < reached - s_next:
+                y2 = ppermute(y2, axis_name="tile", perm=cards)
+                value_now = lax.dynamic_update_slice_in_dim(
+                    value_now, y2, (carry_out + no) % reached * block_last, axis=0
+                )
+            no = no + 1
+        return value_now
+
+    return product(matrix, rails_return_all(local_rows))
 
 
 def pair_quarters(stacked, quarter):

time: 389 us -> 385 us (0.990)
  waiting for transfers between devices: 265 us -> 236 us
  local copies, waits for them, and re-layouts: 8.67 us -> 30.9 us
  starting transfers between devices: 6.48 us -> 20.4 us
  matrix products: 51.3 us -> 39.3 us
    all_gather x4 -> x0, waiting for transfers between devices: 144 us -> none  [apply_rows(): lax.all_gather(local_rows, 'tile', axis=0, tiled=True)]
    ppermute x0 -> x12, waiting for transfers between devices: none -> 116 us  [the longest x8 83.1 us: rails_return_all(): v_next = ppermute(v_next, axis_name='tile', perm=arrivals)]
    ppermute x0 -> x12, starting transfers between devices: none -> 14 us  [the longest x4 8.39 us: rails_return_all(): y2 = ppermute(y2, axis_name='tile', perm=cards)]
    dot_general x8, matrix products: 51.3 us -> 39.3 us  [product(): jnp.dot(matrix, vector, preferred_element_type=jnp.float32, precision=lax...]
    dynamic_update_slice x0 -> x14, local copies, waits for them, and re-layouts: none -> 9.08 us  [the longest x8 5.09 us: rails_return_all(): lax.dynamic_update_slice_in_dim(value_now, v_next, (carry_out - no) % rea...]
    ppermute x0 -> x6, local copies, waits for them, and re-layouts: none -> 6.69 us  [the longest x4 4.46 us: rails_return_all(): v_next = ppermute(v_next, axis_name='tile', perm=arrivals)]
  transfers between devices with their start and end apart: 13 -> 21, of which waited for: 13 -> 21; matrix products, arithmetic and copies ran while one was open for 0% -> 4% of each run, Pallas kernels for 0% -> 0%
where the time goes in v1:
time: 385 us; the launch traced here: 384 us
  waiting for transfers between devices  236 us (61%)
  matrix products  39.3 us (10%)
  blocking collectives  38.3 us (10%)
  local copies, waits for them, and re-layouts  30.9 us (8%)
  starting transfers between devices  20.4 us (5%)
  between operations  15.1 us (4%)
  other arithmetic  4.42 us (1%)
    ppermute x8, waiting for transfers between devices, partner_2(): return lax.ppermute(block, axis, route)  84.6 us
    ppermute x8, waiting for transfers between devices, rails_return_all(): v_next = ppermute(v_next, axis_name='tile', perm=arrivals)  83.1 us
    dot_general x8, matrix products, product(): jnp.dot(matrix, vector, preferred_element_type=jnp.float32, precision=lax...  39.3 us
    all_gather x3, blocking collectives, assemble(): whole_quarter = lax.all_gather(block, 'tile', axis=0, tiled=True)  38.3 us
    reduce_scatter x1, waiting for transfers between devices, local(): lax.psum_scatter(product(selector, update), 'tile', scatter_dimension=0,...  35.5 us
    ppermute x4, waiting for transfers between devices, rails_return_all(): y2 = ppermute(y2, axis_name='tile', perm=cards)  32.8 us
    ppermute x4, starting transfers between devices, rails_return_all(): y2 = ppermute(y2, axis_name='tile', perm=cards)  8.39 us
  transfers between devices with their start and end apart: 21, of which 21 were waited for; matrix products, arithmetic and copies ran while one was open for 4% of the time, Pallas kernels for 0%

profile of v1, /device:TPU:0, one launch (start us, length us, event | category | flops | bytes accessed | tf_op | source)
XLA Modules:
  0.0 384.4 jit_solution(5707614444389954158)
XLA Ops:
  7.2 3.0 collective-permute-start
  10.2 1.0 collective-permute-start.1
  11.2 13.0 %collective-permute-done = f32[512,256]{1,0:T(8,128)} collective-permute-done((f32[512,256]{1,0:T(8,128)}, f32[512,256]{1,0:T(8,128)}, u32[]{:S(2)}, u32[]{:S(2)}) %collective-permute-start) | collective-permute-done | bytes 524320 | tf_op jit(solution)/shard_map/ppermute | solution.py:44
  24.2 1.1 collective-permute-start.2
  25.3 2.0 copy.25
  27.6 0.8 copy-done.4
  28.5 2.0 copy.26
  30.5 5.5 %collective-permute-done.1 = f32[512,256]{1,0:T(8,128)} collective-permute-done((f32[512,256]{1,0:T(8,128)}, f32[512,256]{1,0:T(8,128)}, u32[]{:S(2)}, u32[]{:S(2)}) %collective-permute-start.1) | collective-permute-done | bytes 524320 | tf_op jit(solution)/shard_map/ppermute | solution.py:49
  36.0 2.0 copy.27
  38.1 1.1 constant_dynamic-update-slice_fusion.14
  39.2 1.1 constant_dynamic-update-slice_fusion.13
  40.3 5.6 %collective-permute-done.2 = f32[512,256]{1,0:T(8,128)} collective-permute-done((f32[512,256]{1,0:T(8,128)}, f32[512,256]{1,0:T(8,128)}, u32[]{:S(2)}, u32[]{:S(2)}) %collective-permute-start.2) | collective-permute-done | bytes 524320 | tf_op jit(solution)/shard_map/ppermute | solution.py:44
  45.9 2.0 copy.28
  47.9 1.1 constant_dynamic-update-slice_fusion.12
  49.3 5.5 %constant_dynamic-update-slice_fusion.11 = (f32[2048,256]{0,1:T(8,128)S(1)}, f32[512,256]{0,1:T(8,128)S(1)}) fusion(f32[2048,256]{0,1:T(8,128)S(1)} %broadcast.99.clone, s32[]{:T(128)S(6)} %select_n.182, f32[2048,256]{0,1:T(8,128)S(1)} %constant_dynamic-update-slice_fusion.12, f32[1,512,2048]{2,1,0:T(8,128)} %param.11), kind=kOutput, calls=%fused_computation.52 | convolution fusion | flops 3221225472 | bytes 7340036 | tf_op jit(solution)/shard_map/dot_general | solution.py:19
  54.8 0.8 collective-permute-start.3
  55.6 2.1 collective-permute-start.4
  57.8 12.8 %collective-permute-done.3 = f32[512,256]{0,1:T(8,128)S(1)} collective-permute-done((f32[512,256]{0,1:T(8,128)S(1)}, f32[512,256]{0,1:T(8,128)S(1)}, u32[]{:S(2)}, u32[]{:S(2)}) %collective-permute-start.3) | collective-permute-done | bytes 524320 | tf_op jit(solution)/shard_map/ppermute | solution.py:44
  72.1 10.0 %collective-permute-done.4 = f32[512,256]{0,1:T(8,128)S(1)} collective-permute-done((f32[512,256]{0,1:T(8,128)S(1)}, f32[512,256]{0,1:T(8,128)S(1)}, u32[]{:S(2)}, u32[]{:S(2)}) %collective-permute-start.4) | collective-permute-done | bytes 524320 | tf_op jit(solution)/shard_map/ppermute | solution.py:49
  82.1 9.2 %collective-permute-done.5 = f32[512,256]{0,1:T(8,128)S(1)} collective-permute-done((f32[512,256]{0,1:T(8,128)S(1)}, f32[512,256]{0,1:T(8,128)S(1)}, u32[]{:S(2)}, u32[]{:S(2)}) %collective-permute-start.5) | collective-permute-done | bytes 524320 | tf_op jit(solution)/shard_map/ppermute | solution.py:44
  91.4 3.7 fusion.21
  95.1 3.3 fusion.11
  98.5 35.5 %reduce-scatter.2.cloned.1.call-done = f32[512,256]{1,0:T(8,128)} async-done(((f32[2048,256]{1,0:T(8,128)}), f32[512,256]{1,0:T(8,128)}) %reduce-scatter.2.cloned.1.call-update) | async-done | bytes 524304 | tf_op jit(solution)/shard_map/reduce_scatter | solution.py:116
  134.0 1.1 constant_dynamic-slice_fusion.1
  135.2 1.5 collective-permute-start.6
  136.9 6.4 %collective-permute-done.6 = f32[2,128,256]{1,2,0:T(8,128)S(1)} collective-permute-done((f32[2,128,256]{1,2,0:T(8,128)S(1)}, f32[2,128,256]{1,2,0:T(8,128)S(1)}, u32[]{:S(2)}, u32[]{:S(2)}) %collective-permute-start.6) | collective-permute-done | bytes 262176 | tf_op jit(solution)/shard_map/ppermute | solution.py:15
  143.6 1.2 collective-permute-done.7
  144.8 14.2 %all-gather = f32[1,512,256]{1,2,0:T(8,128)S(1)} all-gather(f32[1,128,256]{1,2,0:T(8,128)S(1)} %add_add_fusion), channel_id=2, replica_groups=mesh['front'=8,'tile'=4] {'tile'}, dimensions={1}, use_global_device_ids=true | all-gather | bytes 655360 | tf_op jit(solution)/shard_map/all_gather | solution.py:72
  159.0 1.9 collective-permute-done.8
  161.1 1.6 collective-permute-start.9
  162.6 23.8 %collective-permute-done.9 = f32[2,512,256]{1,2,0:T(8,128)} collective-permute-done((f32[2,512,256]{1,2,0:T(8,128)S(1)}, f32[2,512,256]{1,2,0:T(8,128)}, u32[]{:S(2)}, u32[]{:S(2)}) %collective-permute-start.9) | collective-permute-done | bytes 1048608 | tf_op jit(solution)/shard_map/ppermute | solution.py:15
  186.5 2.7 maximum_select_fusion
  189.2 1.9 copy.32
  191.0 5.0 %convolution_bitcast_fusion = f32[128,256]{0,1:T(8,128)S(1)} fusion(f32[2048,256]{1,0:T(8,128)} %bitcast.69, f32[1,128,2048]{2,1,0:T(8,128)S(1)} %copy-done), kind=kOutput, calls=%fused_computation.25 | convolution fusion | flops 805306368 | bytes 3276800 | tf_op jit(solution)/shard_map/dot_general | solution.py:19
  196.0 11.5 %all_gather.10 = f32[512,256]{0,1:T(8,128)S(1)} all-gather(f32[128,256]{0,1:T(8,128)S(1)} %convolution_bitcast_fusion), channel_id=1, replica_groups=mesh['front'=8,'tile'=4] {'tile'}, dimensions={0}, use_global_device_ids=true | all-gather | bytes 655360 | tf_op jit(solution)/shard_map/all_gather | solution.py:72
  207.6 1.9 collective-permute-done.10
  209.6 1.5 collective-permute-start.11
  211.1 23.7 %collective-permute-done.11 = f32[2,512,256]{1,2,0:T(8,128)S(1)} collective-permute-done((f32[2,512,256]{1,2,0:T(8,128)S(1)}, f32[2,512,256]{1,2,0:T(8,128)S(1)}, u32[]{:S(2)}, u32[]{:S(2)}) %collective-permute-start.11) | collective-permute-done | bytes 1048608 | tf_op jit(solution)/shard_map/ppermute | solution.py:15
  235.2 1.9 copy.33
  237.0 5.0 %fusion.33 = f32[256,128]{1,0:T(8,128)S(1)} fusion(f32[2048,256]{1,0:T(8,128)} %bitcast.70, f32[1,128,2048]{2,1,0:T(8,128)S(1)} %copy-done.7), kind=kOutput, calls=%fused_computation.29 | convolution fusion | flops 805306368 | bytes 3276800 | tf_op jit(solution)/shard_map/dot_general | solution.py:19
  242.0 12.5 %all_gather.11 = f32[512,256]{0,1:T(8,128)S(1)} all-gather(f32[128,256]{0,1:T(8,128)S(1)} %bitcast.76), channel_id=1, replica_groups=mesh['front'=8,'tile'=4] {'tile'}, dimensions={0}, use_global_device_ids=true | all-gather | bytes 655360 | tf_op jit(solution)/shard_map/all_gather | solution.py:72
  254.6 1.9 collective-permute-done.12
  256.6 1.6 collective-permute-start.13
  258.2 23.7 %collective-permute-done.13 = f32[2,512,256]{1,2,0:T(8,128)S(1)} collective-permute-done((f32[2,512,256]{1,2,0:T(8,128)S(1)}, f32[2,512,256]{1,2,0:T(8,128)S(1)}, u32[]{:S(2)}, u32[]{:S(2)}) %collective-permute-start.13) | collective-permute-done | bytes 1048608 | tf_op jit(solution)/shard_map/ppermute | solution.py:15
  282.2 1.9 copy.34
  284.1 4.0 %fusion.9 = f32[512,256]{1,0:T(8,128)S(1)} fusion(f32[2048,256]{1,0:T(8,128)} %bitcast.75, s32[512]{0:T(512)S(1)} %bitcast.82, pred[512]{0:T(512)(128)(4,1)S(1)} %add_compare_fusion), kind=kOutput, calls=%fused_computation.11 | convolution fusion | flops 3223322624 | bytes 2624000 | tf_op jit(solution)/shard_map/dot_general | solution.py:19
  288.7 2.3 collective-permute-start.15
  291.0 12.8 %collective-permute-done.14 = f32[512,256]{1,0:T(8,128)S(1)} collective-permute-done((f32[512,256]{1,0:T(8,128)S(1)}, f32[512,256]{1,0:T(8,128)S(1)}, u32[]{:S(2)}, u32[]{:S(2)}) %collective-permute-start.14) | collective-permute-done | bytes 524320 | tf_op jit(solution)/shard_map/ppermute | solution.py:44
  304.1 1.6 broadcast.99.clone.2
  305.7 0.9 constant_dynamic-update-slice_fusion.7
  306.8 7.5 %collective-permute-done.15 = f32[512,256]{1,0:T(8,128)S(1)} collective-permute-done((f32[512,256]{1,0:T(8,128)S(1)}, f32[512,256]{1,0:T(8,128)S(1)}, u32[]{:S(2)}, u32[]{:S(2)}) %collective-permute-start.15) | collective-permute-done | bytes 524320 | tf_op jit(solution)/shard_map/ppermute | solution.py:49
  314.5 0.9 constant_dynamic-update-slice_fusion.6
  315.3 0.9 constant_dynamic-update-slice_fusion.5
  316.2 8.4 %collective-permute-done.16 = f32[512,256]{1,0:T(8,128)S(1)} collective-permute-done((f32[512,256]{1,0:T(8,128)S(1)}, f32[512,256]{1,0:T(8,128)S(1)}, u32[]{:S(2)}, u32[]{:S(2)}) %collective-permute-start.16) | collective-permute-done | bytes 524320 | tf_op jit(solution)/shard_map/ppermute | solution.py:44
  324.8 0.9 constant_dynamic-update-slice_fusion.4
  325.9 6.0 %constant_dynamic-update-slice_fusion.3 = (f32[2048,256]{0,1:T(8,128)S(1)}, f32[512,256]{0,1:T(8,128)S(1)}) fusion(f32[2048,256]{0,1:T(8,128)S(1)} %broadcast.99, s32[]{:T(128)S(6)} %select_n.182, f32[512,256]{0,1:T(8,128)S(1)} %copy-done.6, f32[2048,256]{0,1:T(8,128)} %constant_dynamic-update-slice_fusion.4, f32[1,512,2048]{2,1,0:T(8,128)} %param.13), kind=kOutput, calls=%fused_computation.41 | convolution fusion | flops 3221356544 | bytes 7864324 | tf_op jit(solution)/shard_map/dot_general | solution.py:19
  332.0 2.9 collective-permute-start.18
  334.9 12.8 %collective-permute-done.17 = f32[512,256]{0,1:T(8,128)S(1)} collective-permute-done((f32[512,256]{0,1:T(8,128)S(1)}, f32[512,256]{0,1:T(8,128)S(1)}, u32[]{:S(2)}, u32[]{:S(2)}) %collective-permute-start.17) | collective-permute-done | bytes 524320 | tf_op jit(solution)/shard_map/ppermute | solution.py:44
  348.6 9.7 %collective-permute-done.18 = f32[512,256]{0,1:T(8,128)} collective-permute-done((f32[512,256]{0,1:T(8,128)S(1)}, f32[512,256]{0,1:T(8,128)}, u32[]{:S(2)}, u32[]{:S(2)}) %collective-permute-start.18) | collective-permute-done | bytes 524320 | tf_op jit(solution)/shard_map/ppermute | solution.py:49
  358.3 1.1 constant_dynamic-update-slice_fusion.1
  359.4 8.3 %collective-permute-done.19 = f32[512,256]{0,1:T(8,128)} collective-permute-done((f32[512,256]{0,1:T(8,128)S(1)}, f32[512,256]{0,1:T(8,128)}, u32[]{:S(2)}, u32[]{:S(2)}) %collective-permute-start.19) | collective-permute-done | bytes 524320 | tf_op jit(solution)/shard_map/ppermute | solution.py:44
  367.7 1.1 constant_dynamic-update-slice_fusion
  368.8 6.8 %fusion.27 = f32[1,512,256]{1,2,0:T(8,128)} fusion(f32[2048,256]{0,1:T(8,128)S(1)} %constant_dynamic-update-slice_fusion, f32[1,512,2048]{2,1,0:T(8,128)} %param.14), kind=kOutput, calls=%fused_computation.23 | convolution fusion | flops 3221225472 | bytes 6815744 | tf_op jit(solution)/shard_map/dot_general | solution.py:19
  375.6 2.0 copy.39
  (54 shorter events, 5.4 us)
Async XLA Ops:
  7.2 183.8 %copy-start = (f32[1,128,2048]{2,1,0:T(8,128)S(1)}, f32[1,128,2048]{2,1,0:T(8,128)}, u32[]{:S(2)}) copy-start(f32[1,128,2048]{2,1,0:T(8,128)} %param.16) | copy-start | bytes 3145732
  7.2 126.8 %reduce-scatter.2.cloned.1.call-start = ((), (), s32[]{:S(2)}) async-start(), calls=%async_computation.1 | async-start | bytes 2621440 | tf_op jit(solution)/shard_map/reduce_scatter | solution.py:116
  7.2 17.0 %collective-permute-start = (f32[512,256]{1,0:T(8,128)}, f32[512,256]{1,0:T(8,128)}, u32[]{:S(2)}, u32[]{:S(2)}) collective-permute-start(f32[512,256]{1,0:T(8,128)} %bitcast.79), channel_id=1, source_target_pairs={{0,1},{1,2},{2,3},{3,0},{4,5},{5,6},{6,7},{7,4},{8,9},{9,10},{10,1... | collective-permute-start | bytes 1572872 | tf_op jit(solution)/shard_map/ppermute | solution.py:44
  10.2 25.8 %collective-permute-start.1 = (f32[512,256]{1,0:T(8,128)}, f32[512,256]{1,0:T(8,128)}, u32[]{:S(2)}, u32[]{:S(2)}) collective-permute-start(f32[512,256]{1,0:T(8,128)} %bitcast.80), channel_id=1, source_target_pairs={{0,3},{1,0},{2,1},{3,2},{4,7},{5,4},{6,5},{7,6},{8,11},{9,8},{10,9... | collective-permute-start | bytes 1572872 | tf_op jit(solution)/shard_map/ppermute | solution.py:49
  24.2 21.6 %collective-permute-start.2 = (f32[512,256]{1,0:T(8,128)}, f32[512,256]{1,0:T(8,128)}, u32[]{:S(2)}, u32[]{:S(2)}) collective-permute-start(f32[512,256]{1,0:T(8,128)} %collective-permute-done), channel_id=1, source_target_pairs={{0,1},{1,2},{2,3},{3,0},{4,5},{5,6},{6,7},{7,4},{8,9},{9,10},{10,1... | collective-permute-start | bytes 1572872 | tf_op jit(solution)/shard_map/ppermute | solution.py:44
  27.4 1.0 copy-start.4
  49.2 42.1 %copy-start.3 = (f32[1,512,2048]{2,1,0:T(8,128)S(1)}, f32[1,512,2048]{2,1,0:T(8,128)}, u32[]{:S(2)}) copy-start(f32[1,512,2048]{2,1,0:T(8,128)} %param.12) | copy-start | bytes 12582916
  54.8 40.3 %copy-start.5 = (f32[512,256]{0,1:T(8,128)}, f32[512,256]{0,1:T(8,128)S(1)}, u32[]{:S(2)}) copy-start(f32[512,256]{0,1:T(8,128)S(1)} %get-tuple-element.11) | copy-start | bytes 1572868
  54.8 15.8 %collective-permute-start.3 = (f32[512,256]{0,1:T(8,128)S(1)}, f32[512,256]{0,1:T(8,128)S(1)}, u32[]{:S(2)}, u32[]{:S(2)}) collective-permute-start(f32[512,256]{0,1:T(8,128)S(1)} %get-tuple-element.11), channel_id=1, source_target_pairs={{0,1},{1,2},{2,3},{3,0},{4,5},{5,6},{6,7},{7,4},{8,9},{9,10},{10,1... | collective-permute-start | bytes 1572872 | tf_op jit(solution)/shard_map/ppermute | solution.py:44
  55.6 26.5 %collective-permute-start.4 = (f32[512,256]{0,1:T(8,128)S(1)}, f32[512,256]{0,1:T(8,128)S(1)}, u32[]{:S(2)}, u32[]{:S(2)}) collective-permute-start(f32[512,256]{0,1:T(8,128)S(1)} %get-tuple-element.11), channel_id=1, source_target_pairs={{0,3},{1,0},{2,1},{3,2},{4,7},{5,4},{6,5},{7,6},{8,11},{9,8},{10,9... | collective-permute-start | bytes 1572872 | tf_op jit(solution)/shard_map/ppermute | solution.py:49
  70.6 20.7 %collective-permute-start.5 = (f32[512,256]{0,1:T(8,128)S(1)}, f32[512,256]{0,1:T(8,128)S(1)}, u32[]{:S(2)}, u32[]{:S(2)}) collective-permute-start(f32[512,256]{0,1:T(8,128)S(1)} %collective-permute-done.3), channel_id=1, source_target_pairs={{0,1},{1,2},{2,3},{3,0},{4,5},{5,6},{6,7},{7,4},{8,9},{9,10},{10,1... | collective-permute-start | bytes 1572872 | tf_op jit(solution)/shard_map/ppermute | solution.py:44
  98.4 45.0 %copy-start.8 = (f32[1,128,256]{2,1,0:T(8,128)S(1)}, f32[1,128,256]{2,1,0:T(8,128)}, u32[]{:S(2)}) copy-start(f32[1,128,256]{2,1,0:T(8,128)} %param.15) | copy-start | bytes 393220
  135.2 8.1 %collective-permute-start.6 = (f32[2,128,256]{1,2,0:T(8,128)S(1)}, f32[2,128,256]{1,2,0:T(8,128)S(1)}, u32[]{:S(2)}, u32[]{:S(2)}) collective-permute-start(f32[2,128,256]{1,2,0:T(8,128)S(1)} %copy.42), channel_id=1, source_target_pairs={{0,8},{8,0},{4,12},{12,4},{16,24},{24,16},{20,28},{28,20},{1,9},{9... | collective-permute-start | bytes 786440 | tf_op jit(solution)/shard_map/ppermute | solution.py:15
  143.4 1.4 collective-permute-start.7
  159.0 1.9 collective-permute-start.8
  161.1 1.6 copy-start.2
  161.1 25.4 %collective-permute-start.9 = (f32[2,512,256]{1,2,0:T(8,128)S(1)}, f32[2,512,256]{1,2,0:T(8,128)}, u32[]{:S(2)}, u32[]{:S(2)}) collective-permute-start(f32[2,512,256]{1,2,0:T(8,128)S(1)} %maximum_select_fusion.3), channel_id=1, source_target_pairs={{0,8},{8,0},{4,12},{12,4},{16,24},{24,16},{20,28},{28,20},{1,9},{9... | collective-permute-start | bytes 3145736 | tf_op jit(solution)/shard_map/ppermute | solution.py:15
  207.6 1.9 collective-permute-start.10
  209.6 25.3 %collective-permute-start.11 = (f32[2,512,256]{1,2,0:T(8,128)S(1)}, f32[2,512,256]{1,2,0:T(8,128)S(1)}, u32[]{:S(2)}, u32[]{:S(2)}) collective-permute-start(f32[2,512,256]{1,2,0:T(8,128)S(1)} %maximum_select_fusion.4), channel_id=1, source_target_pairs={{0,8},{8,0},{4,12},{12,4},{16,24},{24,16},{20,28},{28,20},{1,9},{9... | collective-permute-start | bytes 3145736 | tf_op jit(solution)/shard_map/ppermute | solution.py:15
  235.2 1.9 copy-start.7
  254.6 1.9 collective-permute-start.12
  256.6 25.3 %collective-permute-start.13 = (f32[2,512,256]{1,2,0:T(8,128)S(1)}, f32[2,512,256]{1,2,0:T(8,128)S(1)}, u32[]{:S(2)}, u32[]{:S(2)}) collective-permute-start(f32[2,512,256]{1,2,0:T(8,128)S(1)} %maximum_select_fusion.5), channel_id=1, source_target_pairs={{0,8},{8,0},{4,12},{12,4},{16,24},{24,16},{20,28},{28,20},{1,9},{9... | collective-permute-start | bytes 3145736 | tf_op jit(solution)/shard_map/ppermute | solution.py:15
  288.1 15.8 %collective-permute-start.14 = (f32[512,256]{1,0:T(8,128)S(1)}, f32[512,256]{1,0:T(8,128)S(1)}, u32[]{:S(2)}, u32[]{:S(2)}) collective-permute-start(f32[512,256]{1,0:T(8,128)S(1)} %fusion.9), channel_id=1, source_target_pairs={{0,1},{1,2},{2,3},{3,0},{4,5},{5,6},{6,7},{7,4},{8,9},{9,10},{10,1... | collective-permute-start | bytes 1572872 | tf_op jit(solution)/shard_map/ppermute | solution.py:44
  288.7 25.5 %collective-permute-start.15 = (f32[512,256]{1,0:T(8,128)S(1)}, f32[512,256]{1,0:T(8,128)S(1)}, u32[]{:S(2)}, u32[]{:S(2)}) collective-permute-start(f32[512,256]{1,0:T(8,128)S(1)} %fusion.9), channel_id=1, source_target_pairs={{0,3},{1,0},{2,1},{3,2},{4,7},{5,4},{6,5},{7,6},{8,11},{9,8},{10,9... | collective-permute-start | bytes 1572872 | tf_op jit(solution)/shard_map/ppermute | solution.py:49
  303.9 20.7 %collective-permute-start.16 = (f32[512,256]{1,0:T(8,128)S(1)}, f32[512,256]{1,0:T(8,128)S(1)}, u32[]{:S(2)}, u32[]{:S(2)}) collective-permute-start(f32[512,256]{1,0:T(8,128)S(1)} %collective-permute-done.14), channel_id=1, source_target_pairs={{0,1},{1,2},{2,3},{3,0},{4,5},{5,6},{6,7},{7,4},{8,9},{9,10},{10,1... | collective-permute-start | bytes 1572872 | tf_op jit(solution)/shard_map/ppermute | solution.py:44
  316.2 9.7 %copy-start.6 = (f32[512,256]{0,1:T(8,128)S(1)}, f32[512,256]{0,1:T(8,128)}, u32[]{:S(2)}) copy-start(f32[512,256]{0,1:T(8,128)} %copy-done.5) | copy-start | bytes 1572868
  332.0 15.8 %collective-permute-start.17 = (f32[512,256]{0,1:T(8,128)S(1)}, f32[512,256]{0,1:T(8,128)S(1)}, u32[]{:S(2)}, u32[]{:S(2)}) collective-permute-start(f32[512,256]{0,1:T(8,128)S(1)} %get-tuple-element.13), channel_id=1, source_target_pairs={{0,1},{1,2},{2,3},{3,0},{4,5},{5,6},{6,7},{7,4},{8,9},{9,10},{10,1... | collective-permute-start | bytes 1572872 | tf_op jit(solution)/shard_map/ppermute | solution.py:44
  332.0 26.3 %collective-permute-start.18 = (f32[512,256]{0,1:T(8,128)S(1)}, f32[512,256]{0,1:T(8,128)}, u32[]{:S(2)}, u32[]{:S(2)}) collective-permute-start(f32[512,256]{0,1:T(8,128)S(1)} %get-tuple-element.13), channel_id=1, source_target_pairs={{0,3},{1,0},{2,1},{3,2},{4,7},{5,4},{6,5},{7,6},{8,11},{9,8},{10,9... | collective-permute-start | bytes 1572872 | tf_op jit(solution)/shard_map/ppermute | solution.py:49
  347.8 19.9 %collective-permute-start.19 = (f32[512,256]{0,1:T(8,128)S(1)}, f32[512,256]{0,1:T(8,128)}, u32[]{:S(2)}, u32[]{:S(2)}) collective-permute-start(f32[512,256]{0,1:T(8,128)S(1)} %collective-permute-done.17), channel_id=1, source_target_pairs={{0,1},{1,2},{2,3},{3,0},{4,5},{5,6},{6,7},{7,4},{8,9},{9,10},{10,1... | collective-permute-start | bytes 1572872 | tf_op jit(solution)/shard_map/ppermute | solution.py:44
  368.8 8.8 %copy-start.1 = (f32[1,128,2048]{2,1,0:T(8,128)S(1)}, f32[1,128,2048]{2,1,0:T(8,128)}, u32[]{:S(2)}) copy-start(f32[1,128,2048]{2,1,0:T(8,128)} %param.16) | copy-start | bytes 3145732
Sparse Core Ops, SparseCore 0:
  98.6 35.3 reduce-scatter.1
